TPU v7x, 32 devices: a whole 2x2x4 slice. The times are simulated.
32 devices in a mesh: grp: 4 (over y, core), blk: 8 (over z, x).
Axes of the slice: x: 2, y: 2, z: 4, core: 2. Of those that a mesh axis runs over, the one named last changes fastest.
Arguments:
- snapshots: float32 [262144, 256], P(('grp', 'blk')), may hold values from -32 to 32, as said below
- start_basis: float32 [256, 32], replicated, may hold values from -6 to 6
Outputs:
- modes: float32 [262144, 32], P(('grp', 'blk'))
- coefficients: float32 [256, 32], replicated
Inputs may be any that keep to these rules, and one draw needn't show every extreme that they name: `snapshots`: real snapshot values of a flow field.
All inputs are finite; a program needn't handle non-finite values.
Results may differ from a plain program's by a relative error of at most 0.0003.
Values sent between devices are 32-bit elements; how exact they have to be, the bound alone decides.
A program may use at most 64 MiB of HBM per device.

v0:
```python
import jax
import jax.numpy as jnp
from jax import lax
from jax.sharding import PartitionSpec as P

HIGH = lax.Precision.HIGHEST


def orthonormal(cols):
    count = cols.shape[1]
    finished_list = []
    for j in range(count):
        vector = cols[:, j]
        if finished_list:
            finished = jnp.stack(finished_list, 0)
            for _ in range(2):
                proj = jnp.dot(finished, vector, precision=HIGH)
                vector = vector - jnp.dot(proj, finished, precision=HIGH)
        vector = vector / jnp.sqrt(jnp.sum(vector * vector) + 1e-06)
        finished_list.append(vector)
    return jnp.stack(finished_list, 1)


def add_outer(piece):
    return jnp.dot(piece, piece.T, precision=HIGH)


def body(snapshots, start_basis):
    points = snapshots.shape[0]
    gram = lax.dot_general(snapshots, snapshots, (((0,), (0,)), ((), ())), precision=HIGH)
    local_basis = orthonormal(jnp.dot(gram, start_basis, precision=HIGH))
    factor = jnp.dot(gram, local_basis, precision=HIGH) / points
    group_gram = add_outer(lax.all_gather(factor, "blk", axis=1, tiled=True))
    group_gram = group_gram / lax.axis_size("blk")
    group_basis = orthonormal(jnp.dot(group_gram, start_basis, precision=HIGH))
    group_factor = jnp.dot(group_gram, group_basis, precision=HIGH)
    total_gram = add_outer(lax.all_gather(group_factor, "grp", axis=1, tiled=True))
    total_gram = total_gram / lax.axis_size("grp")
    coefficients = orthonormal(jnp.dot(total_gram, start_basis, precision=HIGH))
    modes = jnp.dot(snapshots, coefficients, precision=HIGH)
    return (modes, coefficients)


def solution(mesh):
    return jax.shard_map(
        body,
        mesh=mesh,
        in_specs=(P(("grp", "blk"), None), P()),
        out_specs=(P(("grp", "blk"), None), P()),
        check_vma=False,
    )
```

profile of v0, /device:TPU:0, one launch (start us, length us, event | category | flops | bytes accessed | tf_op | source)
XLA Modules:
  0.0 270.4 jit_solution(10377154024828172704)
XLA Ops:
  0.6 19.4 %fusion.99 = f32[256,256]{1,0:T(8,128)S(1)} fusion(f32[8192,256]{1,0:T(8,128)} %param.2), kind=kOutput, calls=%fused_computation.496 | convolution fusion | flops 6442450944 | bytes 8650752 | tf_op jit(solution)/shard_map/dot_general | solution.py:30
  22.4 1.2 multiply_reduce_fusion.4
  23.6 2.0 multiply_reduce_fusion.100
  26.3 1.3 broadcast_divide_fusion.92
  72.7 0.6 multiply_reduce_fusion.76
  74.8 0.6 multiply_reduce_fusion.75
  76.8 0.6 multiply_reduce_fusion.74
  78.8 0.6 multiply_reduce_fusion.73
  80.8 0.6 multiply_reduce_fusion.72
  82.8 0.6 multiply_reduce_fusion.71
  84.8 0.6 multiply_reduce_fusion.70
  86.5 32.7 %all_gather.6 = f32[256,256]{0,1:T(8,128)S(1)} all-gather(f32[256,32]{0,1:T(8,128)S(1)} %convolution_multiply_fusion.2), channel_id=1, replica_groups=mesh['grp'=4,'blk'=8] {'blk'}, dimensions={1}, use_global_device_ids=true | all-gather | bytes 294912 | tf_op jit(solution)/shard_map/all_gather | solution.py:33
  122.2 1.2 multiply_reduce_fusion.2
  123.4 2.0 multiply_reduce_fusion.68
  126.1 1.3 broadcast_divide_fusion.61
  172.5 0.6 multiply_reduce_fusion.44
  174.5 0.6 multiply_reduce_fusion.43
  176.6 0.6 multiply_reduce_fusion.42
  178.6 0.6 multiply_reduce_fusion.41
  180.6 0.6 multiply_reduce_fusion.40
  182.6 0.6 multiply_reduce_fusion.39
  184.6 0.6 multiply_reduce_fusion.38
  186.3 5.7 %all_gather.7 = f32[256,128]{0,1:T(8,128)S(1)} all-gather(f32[256,32]{0,1:T(8,128)S(1)} %fusion.218), channel_id=1, replica_groups=mesh['grp'=4,'blk'=8] {'grp'}, dimensions={1}, use_global_device_ids=true | all-gather | bytes 163840 | tf_op jit(solution)/shard_map/all_gather | solution.py:37
  194.7 1.2 multiply_reduce_fusion
  196.0 2.0 multiply_reduce_fusion.36
  198.7 1.3 broadcast_divide_fusion.30
  245.1 0.6 multiply_reduce_fusion.12
  247.1 0.6 multiply_reduce_fusion.11
  249.1 0.6 multiply_reduce_fusion.10
  251.1 0.6 multiply_reduce_fusion.9
  255.1 0.6 multiply_reduce_fusion.7
  258.5 11.9 %convolution_bitcast_fusion = f32[8192,32]{0,1:T(8,128)} fusion(f32[256,32]{0,1:T(8,128)S(1)} %stack.827, f32[8192,256]{1,0:T(8,128)} %param.2), kind=kOutput, calls=%fused_computation | convolution fusion | flops 805306368 | bytes 9469952 | tf_op jit(solution)/shard_map/dot_general | solution.py:40
  (721 shorter events, 106.8 us)
Async XLA Ops:
  0.6 19.5 %copy-start = (f32[256,32]{0,1:T(8,128)S(1)}, f32[256,32]{0,1:T(8,128)}, u32[]{:S(2)}) copy-start(f32[256,32]{0,1:T(8,128)} %param.3) | copy-start | bytes 98308
  258.5 11.9 %copy-start.1 = (f32[256,32]{0,1:T(8,128)}, f32[256,32]{0,1:T(8,128)S(1)}, u32[]{:S(2)}) copy-start(f32[256,32]{0,1:T(8,128)S(1)} %stack.827) | copy-start | bytes 98308
where the time goes:
time: 272 us; the launch traced here: 270 us
  matrix products  83.3 us (31%)
  other arithmetic  74.1 us (27%)
  between operations  68.5 us (25%)
  blocking collectives  38.4 us (14%)
  local copies, waits for them, and re-layouts  6.13 us (2%)
    reduce_sum x93, other arithmetic, orthonormal(): vector = vector / jnp.sqrt(jnp.sum(vector * vector) + 1e-06)  61.7 us
    all_gather x1, blocking collectives, body(): group_gram = add_outer(lax.all_gather(factor, 'blk', axis=1, tiled=True))  32.7 us
    dot_general x180, matrix products, orthonormal(): proj = jnp.dot(finished, vector, precision=HIGH)  24.7 us
    dot_general x180, matrix products, orthonormal(): vector = vector - jnp.dot(proj, finished, precision=HIGH)  24.5 us
    dot_general x1, matrix products, body(): lax.dot_general(snapshots, snapshots, (((0,), (0,)), ((), ())), precision...  19.4 us
    dot_general x1, matrix products, body(): modes = jnp.dot(snapshots, coefficients, precision=HIGH)  11.9 us
    another operation x81, local copies, waits for them, and re-layouts, orthonormal(): finished = jnp.stack(finished_list, 0)  5.81 us
    all_gather x1, blocking collectives, body(): lax.all_gather(group_factor, 'grp', axis=1, tiled=True)  5.69 us

commit v1 on v0

v1 whole, which is shorter than its diff:
```python
import functools

import jax
import jax.numpy as jnp
from jax import lax
from jax.experimental import pallas as pl
from jax.experimental.pallas import tpu as pltpu
from jax.sharding import PartitionSpec as P

HIGH = lax.Precision.HIGHEST
F32 = jnp.float32
BF16 = jnp.bfloat16
MESH = pl.DeviceIdType.MESH
EPS = 1e-06
CHUNKS = 8


def product(a, b, contract, precision=HIGH):
    return lax.dot_general(
        a, b, (contract, ((), ())), precision=precision, preferred_element_type=F32
    )


def lane_sum(x):
    return jnp.sum(x, axis=1, keepdims=True)


def orthonormal_rows(rows_ref):
    rows = rows_ref[...]
    count = rows.shape[0]
    index = lax.broadcasted_iota(jnp.int32, (count, 1), 0)

    def step(j, state):
        done, left, vector, ahead, leak = state
        following = rows_ref[pl.ds(jnp.minimum(j + 1, count - 1), 1), :]
        overlap = lane_sum(done * vector)
        cross = lane_sum(rows * vector)
        size = lane_sum(vector * vector)
        near = lane_sum(vector * ahead)
        along = lane_sum(vector * following)
        scale = 1.0 / jnp.sqrt(size + EPS)
        unit = vector * scale
        first = along * scale
        second = leak - (first * scale) * overlap
        own = near * scale - first * (scale * scale * size)
        new_vector = (
            ahead
            - unit * (first + own)
            - jnp.sum(done * second, axis=0, keepdims=True)
        )
        new_left = left - unit * (cross * scale)
        new_ahead = jnp.sum(
            jnp.where(index == j + 2, new_left, 0.0), axis=0, keepdims=True
        )
        new_done = jnp.where(index == j, unit, done)
        new_leak = lane_sum(new_done * new_ahead)
        return new_done, new_left, new_vector, new_ahead, new_leak

    state = (
        jnp.zeros_like(rows),
        rows,
        rows[0:1],
        rows[1:2],
        jnp.zeros((count, 1), F32),
    )
    return lax.fori_loop(0, count, step, state)[0]


def kernel(
    n_blk,
    n_grp,
    snap_ref,
    start_ref,
    modes_ref,
    coef_ref,
    snap,
    high,
    low,
    gram,
    rows_ref,
    factors,
    groups,
    load_sem,
    blk_send,
    blk_recv,
    grp_send,
    grp_recv,
):
    points = snap_ref.shape[0]
    count = start_ref.shape[0]
    chunk = points // CHUNKS
    size = snap_ref.shape[1]

    loads = [
        pltpu.make_async_copy(
            snap_ref.at[pl.ds(i * chunk, chunk), :],
            snap.at[pl.ds(i * chunk, chunk), :],
            load_sem.at[i],
        )
        for i in range(CHUNKS)
    ]
    for load in loads:
        load.start()

    me_blk = lax.axis_index("blk")
    me_grp = lax.axis_index("grp")
    barrier = pltpu.get_barrier_semaphore()
    for o in range(1, n_blk):
        peer = lax.rem(me_blk + o, n_blk)
        pl.semaphore_signal(
            barrier, inc=1, device_id={"blk": peer}, device_id_type=MESH
        )
    for o in range(1, n_grp):
        peer = lax.rem(me_grp + o, n_grp)
        pl.semaphore_signal(
            barrier, inc=1, device_id={"grp": peer}, device_id_type=MESH
        )

    def exchange(axis, n, me, buffer, send_sem, recv_sem):
        copies = []
        for o in range(1, n):
            copy = pltpu.make_async_remote_copy(
                src_ref=buffer.at[me],
                dst_ref=buffer.at[me],
                send_sem=send_sem.at[o],
                recv_sem=recv_sem.at[o],
                device_id={axis: lax.rem(me + o, n)},
                device_id_type=MESH,
            )
            copy.start()
            copies.append(copy)
        for o in range(1, n):
            source = lax.rem(me + n - o, n)
            pltpu.make_async_remote_copy(
                src_ref=buffer.at[source],
                dst_ref=buffer.at[source],
                send_sem=send_sem.at[o],
                recv_sem=recv_sem.at[o],
                device_id={axis: lax.rem(me + o, n)},
                device_id_type=MESH,
            ).wait_recv()
        return copies

    gram[...] = jnp.zeros_like(gram)
    for i in range(CHUNKS):
        loads[i].wait()
        part = pl.ds(i * chunk, chunk)
        x = snap[part, :]
        x_high = x.astype(BF16)
        x_low = (x - x_high.astype(F32)).astype(BF16)
        high[part, :] = x_high
        low[part, :] = x_low
        pair = jnp.concatenate([x_high, x_low], axis=1)
        gram[...] += product(x_high, pair, ((0,), (0,)), None)
    mixed = gram[:, size:]
    full = gram[:, :size] + (mixed + mixed.T)

    start = start_ref[...]
    rows_ref[...] = product(start, full, ((1,), (0,)))
    basis = orthonormal_rows(rows_ref)
    factors[me_blk] = product(basis, full, ((1,), (0,))) * (1.0 / points)
    pl.semaphore_wait(barrier, n_blk - 1 + n_grp - 1)
    sent = exchange("blk", n_blk, me_blk, factors, blk_send, blk_recv)

    stacked = factors[...].reshape(n_blk * count, size)
    group_gram = product(stacked, stacked, ((0,), (0,))) * (1.0 / n_blk)
    rows_ref[...] = product(start, group_gram, ((1,), (0,)))
    basis = orthonormal_rows(rows_ref)
    groups[me_grp] = product(basis, group_gram, ((1,), (0,)))
    sent += exchange("grp", n_grp, me_grp, groups, grp_send, grp_recv)

    stacked = groups[...].reshape(n_grp * count, size)
    inner = product(start, stacked, ((1,), (1,)))
    rows_ref[...] = product(inner, stacked, ((1,), (0,))) * (1.0 / n_grp)
    coef = orthonormal_rows(rows_ref)
    coef_ref[...] = coef

    c_high = coef.astype(BF16)
    c_low = (coef - c_high.astype(F32)).astype(BF16)
    pair = jnp.concatenate([c_high, c_low], axis=0)
    for i in range(CHUNKS):
        part = pl.ds(i * chunk, chunk)
        two = product(pair, high[part, :], ((1,), (1,)), None)
        one = product(c_high, low[part, :], ((1,), (1,)), None)
        modes_ref[:, part] = two[:count] + (two[count:] + one)
    for copy in sent:
        copy.wait_send()


def body(n_blk, n_grp, snapshots, start_basis):
    points, size = snapshots.shape
    count = start_basis.shape[1]
    vmem = pl.BlockSpec(memory_space=pltpu.VMEM)
    modes, coef = pl.pallas_call(
        functools.partial(kernel, n_blk, n_grp),
        out_shape=(
            jax.ShapeDtypeStruct((count, points), F32),
            jax.ShapeDtypeStruct((count, size), F32),
        ),
        in_specs=[pl.BlockSpec(memory_space=pltpu.HBM), vmem],
        out_specs=(vmem, vmem),
        scratch_shapes=[
            pltpu.VMEM((points, size), F32),
            pltpu.VMEM((points, size), BF16),
            pltpu.VMEM((points, size), BF16),
            pltpu.VMEM((size, 2 * size), F32),
            pltpu.VMEM((count, size), F32),
            pltpu.VMEM((n_blk, count, size), F32),
            pltpu.VMEM((n_grp, count, size), F32),
            pltpu.SemaphoreType.DMA((CHUNKS,)),
            pltpu.SemaphoreType.DMA((n_blk,)),
            pltpu.SemaphoreType.DMA((n_blk,)),
            pltpu.SemaphoreType.DMA((n_grp,)),
            pltpu.SemaphoreType.DMA((n_grp,)),
        ],
        compiler_params=pltpu.CompilerParams(
            collective_id=0, has_side_effects=True, vmem_limit_bytes=44 * 2**20
        ),
        name="pod",
    )(snapshots, start_basis.T)
    return modes.T, coef.T


def solution(mesh):
    return jax.shard_map(
        functools.partial(body, mesh.shape["blk"], mesh.shape["grp"]),
        mesh=mesh,
        in_specs=(P(("grp", "blk"), None), P()),
        out_specs=(P(("grp", "blk"), None), P()),
        check_vma=False,
    )
```

time: 272 us -> 46.4 us (0.17)
  matrix products: 83.3 us -> 0 us
  other arithmetic: 74.1 us -> 0 us
  between operations: 68.5 us -> 0.65 us
  Pallas kernels: 0 us -> 39.8 us
  blocking collectives: 38.4 us -> 0 us
    dot_general x369 -> x0, matrix products: 83.3 us -> none  [the longest x180 24.7 us: orthonormal(): proj = jnp.dot(finished, vector, precision=HIGH)]
    reduce_sum x93 -> x0, other arithmetic: 61.7 us -> none  [orthonormal(): vector = vector / jnp.sqrt(jnp.sum(vector * vector) + 1e-06)]
    pallas_call x0 -> x1, Pallas kernels: none -> 39.8 us  [body(): pl.pallas_call(functools.partial(kernel, n_blk, n_grp), out_shape=(jax.Sh...]
    all_gather x2 -> x0, blocking collectives: 38.4 us -> none  [the longest x1 32.7 us: body(): group_gram = add_outer(lax.all_gather(factor, 'blk', axis=1, tiled=True))]
    another operation x84 -> x0, local copies, waits for them, and re-layouts: 6.12 us -> none  [the longest x81 5.81 us: orthonormal(): finished = jnp.stack(finished_list, 0)]
    unnamed x4 -> x6, local copies, waits for them, and re-layouts: 0.01 us -> 5.72 us
    dot_general x6 -> x0, other arithmetic: 5.54 us -> none  [orthonormal(): proj = jnp.dot(finished, vector, precision=HIGH)]
    div x93 -> x0, other arithmetic: 4.33 us -> none  [orthonormal(): vector = vector / jnp.sqrt(jnp.sum(vector * vector) + 1e-06)]
where the time goes in v1:
time: 46.4 us; the launch traced here: 46.2 us
  Pallas kernels  39.8 us (86%)
  local copies, waits for them, and re-layouts  5.72 us (12%)
  between operations  0.65 us (1%)
    pallas_call x1, Pallas kernels, body(): pl.pallas_call(functools.partial(kernel, n_blk, n_grp), out_shape=(jax.Sh...  39.8 us
    unnamed x6, local copies, waits for them, and re-layouts  5.72 us

profile of v1, /device:TPU:0, one launch (start us, length us, event | category | flops | bytes accessed | tf_op | source)
XLA Modules:
  0.0 46.2 jit_solution(10190786690075251160)
XLA Ops:
  0.6 0.0 copy-start
  0.6 3.4 %copy-done = f32[8192,256]{1,0:T(8,128)S(1)} copy-done((f32[8192,256]{1,0:T(8,128)S(1)}, f32[8192,256]{1,0:T(8,128)}, u32[]{:S(2)}) %copy-start) | copy-done | bytes 8388632
  4.0 0.0 copy-start.1
  4.0 0.8 %copy-done.1 = f32[256,32]{0,1:T(8,128)S(1)} copy-done((f32[256,32]{0,1:T(8,128)S(1)}, f32[256,32]{0,1:T(8,128)}, u32[]{:S(2)}) %copy-start.1) | copy-done | bytes 32792
  4.8 39.8 %pod.1 = (f32[32,8192]{1,0:T(8,128)S(1)}, f32[32,256]{1,0:T(8,128)S(1)}) custom-call(f32[8192,256]{1,0:T(8,128)S(1)} %copy-done, f32[32,256]{1,0:T(8,128)S(1)} %bitcast.4), custom_call_target="tpu_custom_call" | custom-call | tf_op jit(solution)/shard_map/pod/pallas_call | solution.py:194
  44.6 1.0 %copy.6 = f32[8192,32]{0,1:T(8,128)} copy(f32[8192,32]{0,1:T(8,128)S(1)} %bitcast.3) | data formatting | bytes 2097152
  45.5 0.6 %copy.7 = f32[256,32]{0,1:T(8,128)} copy(f32[256,32]{0,1:T(8,128)S(1)} %bitcast.5) | data formatting | bytes 65536
Async XLA Ops:
  0.6 3.4 %copy-start = (f32[8192,256]{1,0:T(8,128)S(1)}, f32[8192,256]{1,0:T(8,128)}, u32[]{:S(2)}) copy-start(f32[8192,256]{1,0:T(8,128)} %snap_ref.1) | copy-start | bytes 25165828
  4.0 0.8 %copy-start.1 = (f32[256,32]{0,1:T(8,128)S(1)}, f32[256,32]{0,1:T(8,128)}, u32[]{:S(2)}) copy-start(f32[256,32]{0,1:T(8,128)} %param.3) | copy-start | bytes 98308

commit v2 on v1

--- a/solution.py
+++ b/solution.py
@@ -25,45 +25,54 @@
     return jnp.sum(x, axis=1, keepdims=True)
 
 
-def orthonormal_rows(rows_ref):
-    rows = rows_ref[...]
+def sublane_sum(x):
+    return jnp.sum(x, axis=0, keepdims=True)
+
+
+def orthonormal_rows(rows):
     count = rows.shape[0]
-    index = lax.broadcasted_iota(jnp.int32, (count, 1), 0)
-
-    def step(j, state):
-        done, left, vector, ahead, leak = state
-        following = rows_ref[pl.ds(jnp.minimum(j + 1, count - 1), 1), :]
-        overlap = lane_sum(done * vector)
-        cross = lane_sum(rows * vector)
+    blocks = count // 8
+    place = lax.broadcasted_iota(jnp.int32, (8, 1), 0)
+    mixed = [rows[8 * b : 8 * b + 8] for b in range(blocks)]
+    left = list(mixed)
+    vector, ahead = rows[0:1], rows[1:2]
+    leak = [None] * blocks
+    for j in range(count):
+        own_block, own_place = divmod(j, 8)
         size = lane_sum(vector * vector)
+        scale = lax.rsqrt(size + EPS)
+        unit = vector * scale
+        if j == count - 1:
+            mixed[own_block] = jnp.where(place == own_place, unit, mixed[own_block])
+            break
+        dots = [lane_sum(block * vector) for block in mixed]
         near = lane_sum(vector * ahead)
-        along = lane_sum(vector * following)
-        scale = 1.0 / jnp.sqrt(size + EPS)
-        unit = vector * scale
-        first = along * scale
-        second = leak - (first * scale) * overlap
+        first = lane_sum(vector * rows[j + 1 : j + 2]) * scale
         own = near * scale - first * (scale * scale * size)
-        new_vector = (
-            ahead
-            - unit * (first + own)
-            - jnp.sum(done * second, axis=0, keepdims=True)
-        )
-        new_left = left - unit * (cross * scale)
-        new_ahead = jnp.sum(
-            jnp.where(index == j + 2, new_left, 0.0), axis=0, keepdims=True
-        )
-        new_done = jnp.where(index == j, unit, done)
-        new_leak = lane_sum(new_done * new_ahead)
-        return new_done, new_left, new_vector, new_ahead, new_leak
-
-    state = (
-        jnp.zeros_like(rows),
-        rows,
-        rows[0:1],
-        rows[1:2],
-        jnp.zeros((count, 1), F32),
-    )
-    return lax.fori_loop(0, count, step, state)[0]
+        new_vector = ahead - unit * (first + own)
+        again = None
+        for b in range((j + 7) // 8):
+            second = dots[b] * (-first * scale)
+            if leak[b] is not None:
+                second = second + leak[b]
+            if 8 * b + 8 > j:
+                second = jnp.where(place < j - 8 * b, second, 0.0)
+            term = mixed[b] * second
+            again = term if again is None else again + term
+        if again is not None:
+            new_vector = new_vector - sublane_sum(again)
+        mixed[own_block] = jnp.where(place == own_place, unit, mixed[own_block])
+        if j + 2 < count:
+            for b in range((j + 2) // 8, blocks):
+                left[b] = left[b] - unit * (dots[b] * scale)
+            b, p = divmod(j + 2, 8)
+            ahead = left[b][p : p + 1]
+            leak = [
+                lane_sum(mixed[b] * ahead) if b <= own_block else None
+                for b in range(blocks)
+            ]
+        vector = new_vector
+    return jnp.concatenate(mixed, axis=0)
 
 
 def kernel(
@@ -77,7 +86,6 @@
     high,
     low,
     gram,
-    rows_ref,
     factors,
     groups,
     load_sem,
@@ -156,23 +164,21 @@
     full = gram[:, :size] + (mixed + mixed.T)
 
     start = start_ref[...]
-    rows_ref[...] = product(start, full, ((1,), (0,)))
-    basis = orthonormal_rows(rows_ref)
+    basis = orthonormal_rows(product(start, full, ((1,), (0,))))
     factors[me_blk] = product(basis, full, ((1,), (0,))) * (1.0 / points)
     pl.semaphore_wait(barrier, n_blk - 1 + n_grp - 1)
     sent = exchange("blk", n_blk, me_blk, factors, blk_send, blk_recv)
 
     stacked = factors[...].reshape(n_blk * count, size)
     group_gram = product(stacked, stacked, ((0,), (0,))) * (1.0 / n_blk)
-    rows_ref[...] = product(start, group_gram, ((1,), (0,)))
-    basis = orthonormal_rows(rows_ref)
+    basis = orthonormal_rows(product(start, group_gram, ((1,), (0,))))
     groups[me_grp] = product(basis, group_gram, ((1,), (0,)))
     sent += exchange("grp", n_grp, me_grp, groups, grp_send, grp_recv)
 
     stacked = groups[...].reshape(n_grp * count, size)
     inner = product(start, stacked, ((1,), (1,)))
-    rows_ref[...] = product(inner, stacked, ((1,), (0,))) * (1.0 / n_grp)
-    coef = orthonormal_rows(rows_ref)
+    total = product(inner, stacked, ((1,), (0,))) * (1.0 / n_grp)
+    coef = orthonormal_rows(total)
     coef_ref[...] = coef
 
     c_high = coef.astype(BF16)
@@ -204,7 +210,6 @@
             pltpu.VMEM((points, size), BF16),
             pltpu.VMEM((points, size), BF16),
             pltpu.VMEM((size, 2 * size), F32),
-            pltpu.VMEM((count, size), F32),
             pltpu.VMEM((n_blk, count, size), F32),
             pltpu.VMEM((n_grp, count, size), F32),
             pltpu.SemaphoreType.DMA((CHUNKS,)),
@@ -214,7 +219,7 @@
             pltpu.SemaphoreType.DMA((n_grp,)),
         ],
         compiler_params=pltpu.CompilerParams(
-            collective_id=0, has_side_effects=True, vmem_limit_bytes=44 * 2**20
+            collective_id=0, has_side_effects=True, vmem_limit_bytes=58 * 2**20
         ),
         name="pod",
     )(snapshots, start_basis.T)

time: 46.4 us -> 38.5 us (0.83)
  Pallas kernels: 39.8 us -> 33.9 us
  local copies, waits for them, and re-layouts: 5.72 us -> 3.64 us
    pallas_call x1, Pallas kernels: 39.8 us -> 33.9 us  [body(): pl.pallas_call(functools.partial(kernel, n_blk, n_grp), out_shape=(jax.Sh...]
    unnamed x6 -> x2, local copies, waits for them, and re-layouts: 5.72 us -> 3.64 us
where the time goes in v2:
time: 38.5 us; the launch traced here: 38.2 us
  Pallas kernels  33.9 us (88%)
  local copies, waits for them, and re-layouts  3.64 us (9%)
  between operations  0.64 us (2%)
    pallas_call x1, Pallas kernels, body(): pl.pallas_call(functools.partial(kernel, n_blk, n_grp), out_shape=(jax.Sh...  33.9 us
    unnamed x2, local copies, waits for them, and re-layouts  3.64 us

profile of v2, /device:TPU:0, one launch (start us, length us, event | category | flops | bytes accessed | tf_op | source)
XLA Modules:
  0.0 38.2 jit_solution(12780160333466890245)
XLA Ops:
  0.6 33.9 %pod.1 = (f32[32,8192]{1,0:T(8,128)}, f32[32,256]{1,0:T(8,128)}) custom-call(f32[8192,256]{1,0:T(8,128)} %snap_ref.1, f32[32,256]{1,0:T(8,128)} %bitcast.4), custom_call_target="tpu_custom_call" | custom-call | tf_op jit(solution)/shard_map/pod/pallas_call | solution.py:200
  34.5 2.3 %copy.6 = f32[8192,32]{0,1:T(8,128)} copy(f32[8192,32]{0,1:T(8,128)} %bitcast.3) | data formatting | bytes 2097152
  36.8 1.4 %copy.7 = f32[256,32]{0,1:T(8,128)} copy(f32[256,32]{0,1:T(8,128)} %bitcast.5) | data formatting | bytes 65536

commit v3 on v2

--- a/solution.py
+++ b/solution.py
@@ -124,30 +124,63 @@
             barrier, inc=1, device_id={"grp": peer}, device_id_type=MESH
         )
 
-    def exchange(axis, n, me, buffer, send_sem, recv_sem):
-        copies = []
+    def send(buffer, slot, send_sem, recv_sem, target):
+        return pltpu.make_async_remote_copy(
+            src_ref=buffer.at[slot],
+            dst_ref=buffer.at[slot],
+            send_sem=send_sem,
+            recv_sem=recv_sem,
+            device_id=target,
+            device_id_type=MESH,
+        )
+
+    def exchange(n, me, buffer, send_sem, recv_sem, axis):
+        inner = 2 if n % 2 == 0 else 1
+        outer = n // inner
+        line = me // inner
+        spot = me % inner
+        across = {axis: line * inner + (inner - 1 - spot)}
+        sent = []
+        for o in range(1, outer):
+            target = {axis: lax.rem(line + o, outer) * inner + spot}
+            sent.append(send(buffer, me, send_sem.at[o], recv_sem.at[o], target))
+        if inner == 2:
+            sent.append(send(buffer, me, send_sem.at[outer], recv_sem.at[outer], across))
+        for copy in sent:
+            copy.start()
+        for o in range(1, outer):
+            source = lax.rem(line + outer - o, outer) * inner
+            slot = source + spot
+            send(buffer, slot, send_sem.at[o], recv_sem.at[o], across).wait_recv()
+            if inner == 2:
+                place = outer + o
+                forward = send(
+                    buffer, slot, send_sem.at[place], recv_sem.at[place], across
+                )
+                forward.start()
+                sent.append(forward)
+        if inner == 2:
+            for o in range(outer):
+                source = lax.rem(line + outer - o, outer) * inner
+                slot = source + 1 - spot
+                place = outer + o
+                send(
+                    buffer, slot, send_sem.at[place], recv_sem.at[place], across
+                ).wait_recv()
+        return sent
+
+    def spread(n, me, buffer, send_sem, recv_sem, axis):
+        sent = []
         for o in range(1, n):
-            copy = pltpu.make_async_remote_copy(
-                src_ref=buffer.at[me],
-                dst_ref=buffer.at[me],
-                send_sem=send_sem.at[o],
-                recv_sem=recv_sem.at[o],
-                device_id={axis: lax.rem(me + o, n)},
-                device_id_type=MESH,
-            )
+            target = {axis: lax.rem(me + o, n)}
+            sent.append(send(buffer, me, send_sem.at[o], recv_sem.at[o], target))
+        for copy in sent:
             copy.start()
-            copies.append(copy)
         for o in range(1, n):
-            source = lax.rem(me + n - o, n)
-            pltpu.make_async_remote_copy(
-                src_ref=buffer.at[source],
-                dst_ref=buffer.at[source],
-                send_sem=send_sem.at[o],
-                recv_sem=recv_sem.at[o],
-                device_id={axis: lax.rem(me + o, n)},
-                device_id_type=MESH,
-            ).wait_recv()
-        return copies
+            slot = lax.rem(me + n - o, n)
+            target = {axis: lax.rem(me + o, n)}
+            send(buffer, slot, send_sem.at[o], recv_sem.at[o], target).wait_recv()
+        return sent
 
     gram[...] = jnp.zeros_like(gram)
     for i in range(CHUNKS):
@@ -167,18 +200,22 @@
     basis = orthonormal_rows(product(start, full, ((1,), (0,))))
     factors[me_blk] = product(basis, full, ((1,), (0,))) * (1.0 / points)
     pl.semaphore_wait(barrier, n_blk - 1 + n_grp - 1)
-    sent = exchange("blk", n_blk, me_blk, factors, blk_send, blk_recv)
+    sent = exchange(n_blk, me_blk, factors, blk_send, blk_recv, "blk")
 
     stacked = factors[...].reshape(n_blk * count, size)
+    inner = product(start, stacked, ((1,), (1,)))
+    columns = product(inner, stacked, ((1,), (0,))) * (1.0 / n_blk)
     group_gram = product(stacked, stacked, ((0,), (0,))) * (1.0 / n_blk)
-    basis = orthonormal_rows(product(start, group_gram, ((1,), (0,))))
-    groups[me_grp] = product(basis, group_gram, ((1,), (0,)))
-    sent += exchange("grp", n_grp, me_grp, groups, grp_send, grp_recv)
-
-    stacked = groups[...].reshape(n_grp * count, size)
-    inner = product(start, stacked, ((1,), (1,)))
-    total = product(inner, stacked, ((1,), (0,))) * (1.0 / n_grp)
-    coef = orthonormal_rows(total)
+    basis = orthonormal_rows(columns)
+    group_factor = product(basis, group_gram, ((1,), (0,)))
+    inner = product(columns, basis, ((1,), (1,)))
+    groups[me_grp] = product(inner, group_factor, ((1,), (0,)))
+    sent += spread(n_grp, me_grp, groups, grp_send, grp_recv, "grp")
+
+    total = groups[0]
+    for g in range(1, n_grp):
+        total = total + groups[g]
+    coef = orthonormal_rows(total * (1.0 / n_grp))
     coef_ref[...] = coef
 
     c_high = coef.astype(BF16)
@@ -219,7 +256,7 @@
             pltpu.SemaphoreType.DMA((n_grp,)),
         ],
         compiler_params=pltpu.CompilerParams(
-            collective_id=0, has_side_effects=True, vmem_limit_bytes=58 * 2**20
+            collective_id=0, has_side_effects=True, vmem_limit_bytes=52 * 2**20
         ),
         name="pod",
     )(snapshots, start_basis.T)

time: 38.5 us -> 36.4 us (0.945)
  local copies, waits for them, and re-layouts: 3.64 us -> 2.34 us
  Pallas kernels: 33.9 us -> 33.3 us
    unnamed x2 -> x4, local copies, waits for them, and re-layouts: 3.64 us -> 2.34 us
    pallas_call x1, Pallas kernels: 33.9 us -> 33.3 us  [body(): pl.pallas_call(functools.partial(kernel, n_blk, n_grp), out_shape=(jax.Sh...]
where the time goes in v3:
time: 36.4 us; the launch traced here: 36.3 us
  Pallas kernels  33.3 us (91%)
  local copies, waits for them, and re-layouts  2.34 us (6%)
  between operations  0.65 us (2%)
    pallas_call x1, Pallas kernels, body(): pl.pallas_call(functools.partial(kernel, n_blk, n_grp), out_shape=(jax.Sh...  33.3 us
    unnamed x4, local copies, waits for them, and re-layouts  2.34 us

profile of v3, /device:TPU:0, one launch (start us, length us, event | category | flops | bytes accessed | tf_op | source)
XLA Modules:
  0.0 36.3 jit_solution(10746916863406826620)
XLA Ops:
  0.6 0.0 copy-start
  0.6 0.7 %copy-done = f32[256,32]{0,1:T(8,128)S(1)} copy-done((f32[256,32]{0,1:T(8,128)S(1)}, f32[256,32]{0,1:T(8,128)}, u32[]{:S(2)}) %copy-start) | copy-done | bytes 32792
  1.4 33.3 %pod.1 = (f32[32,8192]{1,0:T(8,128)S(1)}, f32[32,256]{1,0:T(8,128)S(1)}) custom-call(f32[8192,256]{1,0:T(8,128)} %snap_ref.1, f32[32,256]{1,0:T(8,128)S(1)} %bitcast.4), custom_call_target="tpu_custom_call" | custom-call | tf_op jit(solution)/shard_map/pod/pallas_call | solution.py:237
  34.7 1.0 %copy.6 = f32[8192,32]{0,1:T(8,128)} copy(f32[8192,32]{0,1:T(8,128)S(1)} %bitcast.3) | data formatting | bytes 2097152
  35.6 0.6 %copy.7 = f32[256,32]{0,1:T(8,128)} copy(f32[256,32]{0,1:T(8,128)S(1)} %bitcast.5) | data formatting | bytes 65536
Async XLA Ops:
  0.6 0.8 %copy-start = (f32[256,32]{0,1:T(8,128)S(1)}, f32[256,32]{0,1:T(8,128)}, u32[]{:S(2)}) copy-start(f32[256,32]{0,1:T(8,128)} %param.3) | copy-start | bytes 98308

commit v4 on v3

--- a/solution.py
+++ b/solution.py
@@ -13,6 +13,7 @@
 MESH = pl.DeviceIdType.MESH
 EPS = 1e-06
 CHUNKS = 8
+PIECES = ((0, 1), (1, 2), (2, 4))
 
 
 def product(a, b, contract, precision=HIGH):
@@ -29,7 +30,7 @@
     return jnp.sum(x, axis=0, keepdims=True)
 
 
-def orthonormal_rows(rows):
+def orthonormal_rows(rows, finished=None):
     count = rows.shape[0]
     blocks = count // 8
     place = lax.broadcasted_iota(jnp.int32, (8, 1), 0)
@@ -44,6 +45,8 @@
         unit = vector * scale
         if j == count - 1:
             mixed[own_block] = jnp.where(place == own_place, unit, mixed[own_block])
+            if finished is not None:
+                finished(own_block, mixed)
             break
         dots = [lane_sum(block * vector) for block in mixed]
         near = lane_sum(vector * ahead)
@@ -62,6 +65,8 @@
         if again is not None:
             new_vector = new_vector - sublane_sum(again)
         mixed[own_block] = jnp.where(place == own_place, unit, mixed[own_block])
+        if own_place == 7 and finished is not None:
+            finished(own_block, mixed)
         if j + 2 < count:
             for b in range((j + 2) // 8, blocks):
                 left[b] = left[b] - unit * (dots[b] * scale)
@@ -88,6 +93,8 @@
     gram,
     factors,
     groups,
+    start_vmem,
+    start_sem,
     load_sem,
     blk_send,
     blk_recv,
@@ -99,6 +106,8 @@
     chunk = points // CHUNKS
     size = snap_ref.shape[1]
 
+    start_load = pltpu.make_async_copy(start_ref, start_vmem, start_sem)
+    start_load.start()
     loads = [
         pltpu.make_async_copy(
             snap_ref.at[pl.ds(i * chunk, chunk), :],
@@ -134,40 +143,17 @@
             device_id_type=MESH,
         )
 
-    def exchange(n, me, buffer, send_sem, recv_sem, axis):
-        inner = 2 if n % 2 == 0 else 1
-        outer = n // inner
-        line = me // inner
-        spot = me % inner
-        across = {axis: line * inner + (inner - 1 - spot)}
-        sent = []
-        for o in range(1, outer):
-            target = {axis: lax.rem(line + o, outer) * inner + spot}
-            sent.append(send(buffer, me, send_sem.at[o], recv_sem.at[o], target))
-        if inner == 2:
-            sent.append(send(buffer, me, send_sem.at[outer], recv_sem.at[outer], across))
-        for copy in sent:
-            copy.start()
-        for o in range(1, outer):
-            source = lax.rem(line + outer - o, outer) * inner
-            slot = source + spot
-            send(buffer, slot, send_sem.at[o], recv_sem.at[o], across).wait_recv()
-            if inner == 2:
-                place = outer + o
-                forward = send(
-                    buffer, slot, send_sem.at[place], recv_sem.at[place], across
-                )
-                forward.start()
-                sent.append(forward)
-        if inner == 2:
-            for o in range(outer):
-                source = lax.rem(line + outer - o, outer) * inner
-                slot = source + 1 - spot
-                place = outer + o
-                send(
-                    buffer, slot, send_sem.at[place], recv_sem.at[place], across
-                ).wait_recv()
-        return sent
+    def send_rows(slot, piece, o):
+        first, last = PIECES[piece]
+        part = factors.at[slot, pl.ds(8 * first, 8 * (last - first)), :]
+        return pltpu.make_async_remote_copy(
+            src_ref=part,
+            dst_ref=part,
+            send_sem=blk_send.at[piece, o],
+            recv_sem=blk_recv.at[piece, o],
+            device_id={"blk": lax.rem(me_blk + o, n_blk)},
+            device_id_type=MESH,
+        )
 
     def spread(n, me, buffer, send_sem, recv_sem, axis):
         sent = []
@@ -196,11 +182,29 @@
     mixed = gram[:, size:]
     full = gram[:, :size] + (mixed + mixed.T)
 
-    start = start_ref[...]
-    basis = orthonormal_rows(product(start, full, ((1,), (0,))))
-    factors[me_blk] = product(basis, full, ((1,), (0,))) * (1.0 / points)
+    start_load.wait()
+    start = start_vmem[...]
+    sent = []
+
+    def factor_rows(block, basis):
+        for piece, (first, last) in enumerate(PIECES):
+            if last != block + 1:
+                continue
+            rows = jnp.concatenate(basis[first:last], axis=0)
+            factors[me_blk, pl.ds(8 * first, 8 * (last - first)), :] = product(
+                rows, full, ((1,), (0,))
+            ) * (1.0 / points)
+            for o in range(1, n_blk):
+                copy = send_rows(me_blk, piece, o)
+                copy.start()
+                sent.append(copy)
+
+    columns = product(start, full, ((1,), (0,)))
     pl.semaphore_wait(barrier, n_blk - 1 + n_grp - 1)
-    sent = exchange(n_blk, me_blk, factors, blk_send, blk_recv, "blk")
+    orthonormal_rows(columns, factor_rows)
+    for piece in range(len(PIECES)):
+        for o in range(1, n_blk):
+            send_rows(lax.rem(me_blk + n_blk - o, n_blk), piece, o).wait_recv()
 
     stacked = factors[...].reshape(n_blk * count, size)
     inner = product(start, stacked, ((1,), (1,)))
@@ -240,7 +244,7 @@
             jax.ShapeDtypeStruct((count, points), F32),
             jax.ShapeDtypeStruct((count, size), F32),
         ),
-        in_specs=[pl.BlockSpec(memory_space=pltpu.HBM), vmem],
+        in_specs=[pl.BlockSpec(memory_space=pltpu.HBM)] * 2,
         out_specs=(vmem, vmem),
         scratch_shapes=[
             pltpu.VMEM((points, size), F32),
@@ -249,9 +253,11 @@
             pltpu.VMEM((size, 2 * size), F32),
             pltpu.VMEM((n_blk, count, size), F32),
             pltpu.VMEM((n_grp, count, size), F32),
+            pltpu.VMEM((count, size), F32),
+            pltpu.SemaphoreType.DMA,
             pltpu.SemaphoreType.DMA((CHUNKS,)),
-            pltpu.SemaphoreType.DMA((n_blk,)),
-            pltpu.SemaphoreType.DMA((n_blk,)),
+            pltpu.SemaphoreType.DMA((len(PIECES), n_blk)),
+            pltpu.SemaphoreType.DMA((len(PIECES), n_blk)),
             pltpu.SemaphoreType.DMA((n_grp,)),
             pltpu.SemaphoreType.DMA((n_grp,)),
         ],

time: 36.4 us -> 35 us (0.962)
  Pallas kernels: 33.3 us -> 31.9 us
    pallas_call x1, Pallas kernels: 33.3 us -> 31.9 us  [body(): pl.pallas_call(functools.partial(kernel, n_blk, n_grp), out_shape=(jax.Sh...]
where the time goes in v4:
time: 35 us; the launch traced here: 34.9 us
  Pallas kernels  31.9 us (91%)
  local copies, waits for them, and re-layouts  2.34 us (7%)
  between operations  0.65 us (2%)
    pallas_call x1, Pallas kernels, body(): pl.pallas_call(functools.partial(kernel, n_blk, n_grp), out_shape=(jax.Sh...  31.9 us
    unnamed x4, local copies, waits for them, and re-layouts  2.34 us

profile of v4, /device:TPU:0, one launch (start us, length us, event | category | flops | bytes accessed | tf_op | source)
XLA Modules:
  0.0 34.9 jit_solution(17395341610277922656)
XLA Ops:
  0.6 0.0 copy-start
  0.6 0.7 %copy-done = f32[256,32]{0,1:T(8,128)S(1)} copy-done((f32[256,32]{0,1:T(8,128)S(1)}, f32[256,32]{0,1:T(8,128)}, u32[]{:S(2)}) %copy-start) | copy-done | bytes 32792
  1.4 31.9 %pod.1 = (f32[32,8192]{1,0:T(8,128)S(1)}, f32[32,256]{1,0:T(8,128)S(1)}) custom-call(f32[8192,256]{1,0:T(8,128)} %snap_ref.1, f32[32,256]{1,0:T(8,128)S(1)} %bitcast.4), custom_call_target="tpu_custom_call" | custom-call | tf_op jit(solution)/shard_map/pod/pallas_call | solution.py:241
  33.3 1.0 %copy.6 = f32[8192,32]{0,1:T(8,128)} copy(f32[8192,32]{0,1:T(8,128)S(1)} %bitcast.3) | data formatting | bytes 2097152
  34.2 0.6 %copy.7 = f32[256,32]{0,1:T(8,128)} copy(f32[256,32]{0,1:T(8,128)S(1)} %bitcast.5) | data formatting | bytes 65536
Async XLA Ops:
  0.6 0.8 %copy-start = (f32[256,32]{0,1:T(8,128)S(1)}, f32[256,32]{0,1:T(8,128)}, u32[]{:S(2)}) copy-start(f32[256,32]{0,1:T(8,128)} %param.3) | copy-start | bytes 98308
